TPU v7x, 512 devices: a whole 4x4x16 slice. The times are simulated.
512 devices in a mesh: slab: 64 (over z, x), sec: 8 (over y, core).
Axes of the slice: x: 4, y: 4, z: 16, core: 2. Of those that a mesh axis runs over, the one named last changes fastest.
Arguments:
- source: float32 [64, 65536], P(None, ('slab', 'sec'))
- fine_blocks: bfloat16 [3, 64, 64, 65536], P(None, None, None, ('slab', 'sec'))
- fine_pattern: int32 [3, 65536], P(None, ('slab', 'sec')), may hold values from 0 to 65535, as said below
- fine_prolong: bfloat16 [3, 64, 6, 65536], P(None, None, None, ('slab', 'sec')), may hold values from -0.75 to 0.75
- prolong_pattern: int32 [3, 65536], P(None, ('slab', 'sec')), may hold values from 0 to 65535, as said below
- coarse_blocks: bfloat16 [3, 6, 6, 65536], P(None, None, None, 'slab')
- coarse_pattern: int32 [3, 65536], P(None, 'slab'), may hold values from 0 to 65535, as said below
- section_prolong: bfloat16 [3, 6, 24, 65536], P(None, None, None, 'slab'), may hold values from -0.046875 to 0.046875
- coarsest_inverse: float32 [1536, 1536], P('slab')
Outputs:
- solution: float32 [64, 65536], P(None, ('slab', 'sec'))
Inputs may be any that keep to these rules, and one draw needn't show every extreme that they name: `fine_pattern`: row 0 names the aggregate itself; the other rows name aggregates at most 96 away, and distance exactly 96 occurs in every draw. `prolong_pattern`: row 0 names the aggregate's own coarse block; the other rows name coarse blocks at most 96 away, and distance exactly 96 occurs in every draw. `coarse_pattern`: row 0 names the block itself; the other rows name coarse blocks at most 96 away, and distance exactly 96 occurs in every draw.
All inputs are finite; a program needn't handle non-finite values.
Results may differ from a plain program's by a relative error of at most 0.0003.
Values sent between devices are 32-bit elements; how exact they have to be, the bound alone decides.
No kernel may reach another device: no remote copies, remote signals or barrier semaphores. Data moves between devices by JAX's collectives and lax.ppermute only.
A program may use at most 64 MiB of HBM per device.

v0:
```python
import jax
import jax.numpy as jnp
from jax import lax
from jax.sharding import PartitionSpec as P

HB = 96
CYCLES = 2
KEEP = 1.0 / 7.0
FRESH = 8.0 / 7.0


def padded(array, sides, width):
    for axis, dim in sides:
        count, length = (lax.axis_size(axis), array.shape[dim])
        up = [(i, (i + 1) % count) for i in range(count - 1)]
        down = [(j, i) for i, j in up]
        last = lax.slice_in_dim(array, length - width, length, axis=dim)
        leading = lax.slice_in_dim(array, 0, width, axis=dim)
        before = lax.ppermute(last, axis, up)
        after = lax.ppermute(leading, axis, down)
        array = jnp.concatenate([before, array, after], axis=dim)
    return array


def from_behind(value, axis, steps):
    count = lax.axis_size(axis)
    leading, last = (max(0, -steps), min(count, count - steps))
    return lax.ppermute(value, axis, [(source, source + steps) for source in range(leading, last)])


def inverse_diagonal(matrix):
    return 1.0 / jnp.diagonal(matrix[0], axis1=0, axis2=1).T.astype(jnp.float32)


def apply_local(matrix, local_cols, extended):
    picked = jnp.swapaxes(extended[:, local_cols], 0, 1)
    return jnp.sum(matrix * picked[:, None, :, :], axis=(0, 2))


def smooth(operator, inverse, rhs, start):
    if start is None:
        change = inverse * rhs
        field = change
    else:
        change = inverse * (rhs - operator(start))
        field = start + change
    change = KEEP * change + FRESH * inverse * (rhs - operator(field))
    return field + change


def shards(
    source,
    fine_blocks,
    fine_pattern,
    fine_prolong,
    prolong_pattern,
    coarse_blocks,
    coarse_pattern,
    section_prolong,
    coarsest_inverse,
):
    reach = HB
    own_rows = source.shape[1]
    section_rows = coarse_blocks.shape[3]
    device = lax.axis_index(("slab", "sec"))
    section = lax.axis_index("slab")
    fine_cols = fine_pattern - (device * own_rows - reach)
    coarse_cols = coarse_pattern - (section * section_rows - reach)
    gather_cols = prolong_pattern - (section * section_rows - reach)
    fine_inverse = inverse_diagonal(fine_blocks)
    coarse_inverse = inverse_diagonal(coarse_blocks)

    def fine_apply(field):
        extended = padded(field, ((("slab", "sec"), 1),), reach)
        return apply_local(fine_blocks, fine_cols, extended)

    def coarse_extend(field):
        return padded(field, (("slab", 1),), reach)

    def coarse_apply(field):
        return apply_local(coarse_blocks, coarse_cols, coarse_extend(field))

    solution = None
    for turn_index in range(CYCLES):
        solution = smooth(fine_apply, fine_inverse, source, solution)
        residual = source - fine_apply(solution)
        terms = jnp.sum(fine_prolong * residual[None, :, None, :], axis=1)
        modes = terms.shape[1]
        flat = jnp.swapaxes(terms, 0, 1).reshape(modes, -1)
        slots = gather_cols.reshape(-1)
        partial_sum = (
            jnp.zeros((modes, section_rows + 2 * reach), jnp.float32).at[:, slots].add(flat)
        )
        partial_sum = lax.psum(partial_sum, "sec")
        lower = from_behind(partial_sum[:, section_rows + reach :], "slab", 1)
        upper = from_behind(partial_sum[:, :reach], "slab", -1)
        inner = partial_sum[:, reach : reach + section_rows]
        coarse_rhs = inner.at[:, :reach].add(lower).at[:, section_rows - reach :].add(upper)
        coarse_sol = smooth(coarse_apply, coarse_inverse, coarse_rhs, None)
        coarse_res = coarse_rhs - coarse_apply(coarse_sol)
        parts = jnp.sum(section_prolong * coarse_res[None, :, None, :], axis=(1, 3))
        width = parts.shape[1]
        every = lax.all_gather(parts[None], "slab", axis=0, tiled=True)
        zero = jnp.zeros((1, width), jnp.float32)
        total = (
            every[:, 1]
            + jnp.concatenate([every[1:, 0], zero], 0)
            + jnp.concatenate([zero, every[:-1, 2]], 0)
        )
        answer = jnp.dot(coarsest_inverse, total.reshape(-1), precision=lax.Precision.HIGHEST)
        nearby = padded(answer[None, :], (("slab", 0),), 1)
        coarse_sol = coarse_sol + jnp.sum(section_prolong * nearby[:, None, :, None], axis=(0, 2))
        coarse_sol = smooth(coarse_apply, coarse_inverse, coarse_rhs, coarse_sol)
        prolong_extended = coarse_extend(coarse_sol)
        picked = jnp.swapaxes(prolong_extended[:, gather_cols], 0, 1)
        solution = solution + jnp.sum(fine_prolong * picked[:, None, :, :], axis=(0, 2))
        solution = smooth(fine_apply, fine_inverse, source, solution)
    return solution


def solution(mesh):
    in_specs = (
        P(None, ("slab", "sec")),
        P(None, None, None, ("slab", "sec")),
        P(None, ("slab", "sec")),
        P(None, None, None, ("slab", "sec")),
        P(None, ("slab", "sec")),
        P(None, None, None, "slab"),
        P(None, "slab"),
        P(None, None, None, "slab"),
        P("slab", None),
    )
    out_specs = P(None, ("slab", "sec"))
    return jax.shard_map(shards, mesh=mesh, in_specs=in_specs, out_specs=out_specs, check_vma=False)
```

profile of v0, /device:TPU:127, one launch (start us, length us, event | category | flops | bytes accessed | tf_op | source)
XLA Modules:
  0.0 759.0 jit_solution(1430777949323937785)
XLA Ops:
  33.6 8.1 %collective-permute-done.3 = f32[64,96]{1,0:T(8,128)S(1)} collective-permute-done((f32[64,96]{1,0:T(8,128)S(1)}, f32[64,96]{1,0:T(8,128)S(1)}, u32[]{:S(2)}, u32[]{:S(2)}) %collective-permute-start.3) | collective-permute-done | bytes 24608 | tf_op jit(solution)/shard_map/ppermute | solution.py:20
  53.9 23.9 %psum.14 = f32[6,1216]{1,0:T(8,128)S(1)} all-reduce(f32[6,1216]{1,0:T(8,128)S(1)} %copy.153), channel_id=1, replica_groups=mesh['slab'=64,'sec'=8] {'sec'}, use_global_device_ids=true, to_apply=%region_4.5 | all-reduce | flops 7296 | bytes 58368 | tf_op jit(solution)/shard_map/psum | solution.py:94
  100.5 11.9 %gather_fusion.4 = f32[3072,6]{1,0:T(8,128)} fusion(f32[6,1216]{0,1:T(8,128)} %copy.154, s32[3072]{0:T(1024)S(1)} %broadcast_clamp_fusion), kind=kCustom, calls=%fused_computation.4 | custom fusion | bytes 159744 | tf_op jit(solution)/shard_map/gather | solution.py:36
  126.3 11.9 %gather_fusion.5 = f32[3072,6]{1,0:T(8,128)} fusion(f32[6,1216]{0,1:T(8,128)} %copy.156, s32[3072]{0:T(1024)S(1)} %broadcast_clamp_fusion), kind=kCustom, calls=%fused_computation.5 | custom fusion | bytes 159744 | tf_op jit(solution)/shard_map/gather | solution.py:36
  142.6 72.8 %all-gather.2 = f32[64,3,24]{2,1,0:T(4,128)S(1)} all-gather(f32[1,3,24]{2,1,0:T(4,128)S(1)} %bitcast.134), channel_id=2, replica_groups=mesh['slab'=64,'sec'=8] {'slab'}, dimensions={0}, use_global_device_ids=true | all-gather | bytes 18720 | tf_op jit(solution)/shard_map/all_gather | solution.py:103
  222.4 5.7 collective-permute-done.11
  240.4 11.9 %gather_fusion.6 = f32[3072,6]{1,0:T(8,128)} fusion(f32[6,1216]{0,1:T(8,128)} %copy.162, s32[3072]{0:T(1024)S(1)} %broadcast_clamp_fusion), kind=kCustom, calls=%fused_computation.6 | custom fusion | bytes 159744 | tf_op jit(solution)/shard_map/gather | solution.py:36
  268.2 11.9 %gather_fusion.7 = f32[3072,6]{1,0:T(8,128)} fusion(f32[6,1216]{0,1:T(8,128)} %copy.164, s32[3072]{0:T(1024)S(1)} %broadcast_clamp_fusion), kind=kCustom, calls=%fused_computation.7 | custom fusion | bytes 159744 | tf_op jit(solution)/shard_map/gather | solution.py:36
  299.4 38.0 %collective-permute-start.18 = (f32[64,96]{1,0:T(8,128)S(1)}, f32[64,96]{1,0:T(8,128)S(1)}, u32[]{:S(2)}, u32[]{:S(2)}) collective-permute-start(f32[64,96]{1,0:T(8,128)S(1)} %get-tuple-element.83), channel_id=1, source_target_pairs={{0,1},{1,2},{2,3},{3,4},{4,5},{5,6},{6,7},{7,8},{8,9},{9,10},{10,1... | collective-permute-start | bytes 73736 | tf_op jit(solution)/shard_map/ppermute | solution.py:19
  339.5 8.5 %collective-permute-done.19 = f32[64,96]{1,0:T(8,128)S(1)} collective-permute-done((f32[64,96]{1,0:T(8,128)S(1)}, f32[64,96]{1,0:T(8,128)S(1)}, u32[]{:S(2)}, u32[]{:S(2)}) %collective-permute-start.19) | collective-permute-done | bytes 24608 | tf_op jit(solution)/shard_map/ppermute | solution.py:20
  357.8 8.2 %collective-permute-done.21 = f32[64,96]{1,0:T(8,128)S(1)} collective-permute-done((f32[64,96]{1,0:T(8,128)S(1)}, f32[64,96]{1,0:T(8,128)S(1)}, u32[]{:S(2)}, u32[]{:S(2)}) %collective-permute-start.21) | collective-permute-done | bytes 24608 | tf_op jit(solution)/shard_map/ppermute | solution.py:20
  375.7 8.2 %collective-permute-done.23 = f32[64,96]{1,0:T(8,128)S(1)} collective-permute-done((f32[64,96]{1,0:T(8,128)S(1)}, f32[64,96]{1,0:T(8,128)S(1)}, u32[]{:S(2)}, u32[]{:S(2)}) %collective-permute-start.23) | collective-permute-done | bytes 24608 | tf_op jit(solution)/shard_map/ppermute | solution.py:20
  396.7 8.2 %collective-permute-done.25 = f32[64,96]{1,0:T(8,128)S(1)} collective-permute-done((f32[64,96]{1,0:T(8,128)S(1)}, f32[64,96]{1,0:T(8,128)S(1)}, u32[]{:S(2)}, u32[]{:S(2)}) %collective-permute-start.25) | collective-permute-done | bytes 24608 | tf_op jit(solution)/shard_map/ppermute | solution.py:20
  417.7 8.2 %collective-permute-done.27 = f32[64,96]{1,0:T(8,128)S(1)} collective-permute-done((f32[64,96]{1,0:T(8,128)S(1)}, f32[64,96]{1,0:T(8,128)S(1)}, u32[]{:S(2)}, u32[]{:S(2)}) %collective-permute-start.27) | collective-permute-done | bytes 24608 | tf_op jit(solution)/shard_map/ppermute | solution.py:20
  440.1 24.5 %psum.15 = f32[6,1216]{1,0:T(8,128)S(1)} all-reduce(f32[6,1216]{1,0:T(8,128)} %copy.179), channel_id=1, replica_groups=mesh['slab'=64,'sec'=8] {'sec'}, use_global_device_ids=true, to_apply=%region_20.21 | all-reduce | flops 7296 | bytes 58368 | tf_op jit(solution)/shard_map/psum | solution.py:94
  485.4 11.9 %gather_fusion.14 = f32[3072,6]{1,0:T(8,128)} fusion(f32[6,1216]{0,1:T(8,128)} %copy.180, s32[3072]{0:T(1024)S(1)} %broadcast_clamp_fusion), kind=kCustom, calls=%fused_computation.14 | custom fusion | bytes 159744 | tf_op jit(solution)/shard_map/gather | solution.py:36
  511.8 11.9 %gather_fusion.15 = f32[3072,6]{1,0:T(8,128)} fusion(f32[6,1216]{0,1:T(8,128)} %copy.182, s32[3072]{0:T(1024)S(1)} %broadcast_clamp_fusion), kind=kCustom, calls=%fused_computation.15 | custom fusion | bytes 159744 | tf_op jit(solution)/shard_map/gather | solution.py:36
  528.8 70.7 %all-gather.3 = f32[64,3,24]{2,1,0:T(4,128)S(1)} all-gather(f32[1,3,24]{2,1,0:T(4,128)S(1)} %bitcast.135), channel_id=3, replica_groups=mesh['slab'=64,'sec'=8] {'slab'}, dimensions={0}, use_global_device_ids=true | all-gather | bytes 18720 | tf_op jit(solution)/shard_map/all_gather | solution.py:103
  609.6 5.7 collective-permute-done.35
  627.6 11.9 %gather_fusion.16 = f32[3072,6]{1,0:T(8,128)} fusion(f32[6,1216]{0,1:T(8,128)} %copy.188, s32[3072]{0:T(1024)S(1)} %broadcast_clamp_fusion), kind=kCustom, calls=%fused_computation.16 | custom fusion | bytes 159744 | tf_op jit(solution)/shard_map/gather | solution.py:36
  655.3 11.9 %gather_fusion.17 = f32[3072,6]{1,0:T(8,128)} fusion(f32[6,1216]{0,1:T(8,128)} %copy.190, s32[3072]{0:T(1024)S(1)} %broadcast_clamp_fusion), kind=kCustom, calls=%fused_computation.17 | custom fusion | bytes 159744 | tf_op jit(solution)/shard_map/gather | solution.py:36
  686.5 38.0 %collective-permute-start.42 = (f32[64,96]{1,0:T(8,128)S(1)}, f32[64,96]{1,0:T(8,128)S(1)}, u32[]{:S(2)}, u32[]{:S(2)}) collective-permute-start(f32[64,96]{1,0:T(8,128)S(1)} %get-tuple-element.63), channel_id=1, source_target_pairs={{0,1},{1,2},{2,3},{3,4},{4,5},{5,6},{6,7},{7,8},{8,9},{9,10},{10,1... | collective-permute-start | bytes 73736 | tf_op jit(solution)/shard_map/ppermute | solution.py:19
  726.5 8.7 %collective-permute-done.43 = f32[64,96]{1,0:T(8,128)S(1)} collective-permute-done((f32[64,96]{1,0:T(8,128)S(1)}, f32[64,96]{1,0:T(8,128)S(1)}, u32[]{:S(2)}, u32[]{:S(2)}) %collective-permute-start.43) | collective-permute-done | bytes 24608 | tf_op jit(solution)/shard_map/ppermute | solution.py:20
  744.9 8.2 %collective-permute-done.45 = f32[64,96]{1,0:T(8,128)S(1)} collective-permute-done((f32[64,96]{1,0:T(8,128)S(1)}, f32[64,96]{1,0:T(8,128)S(1)}, u32[]{:S(2)}, u32[]{:S(2)}) %collective-permute-start.45) | collective-permute-done | bytes 24608 | tf_op jit(solution)/shard_map/ppermute | solution.py:20
  (303 shorter events, 316.9 us)
Async XLA Ops:
  4.9 11.6 %collective-permute-start = (f32[64,96]{1,0:T(8,128)S(1)}, f32[64,96]{1,0:T(8,128)S(1)}, u32[]{:S(2)}, u32[]{:S(2)}) collective-permute-start(f32[64,96]{1,0:T(8,128)S(1)} %get-tuple-element.97), channel_id=1, source_target_pairs={{0,1},{1,2},{2,3},{3,4},{4,5},{5,6},{6,7},{7,8},{8,9},{9,10},{10,1... | collective-permute-start | bytes 73736 | tf_op jit(solution)/shard_map/ppermute | solution.py:19
  9.8 10.7 %collective-permute-start.1 = (f32[64,96]{1,0:T(8,128)S(1)}, f32[64,96]{1,0:T(8,128)S(1)}, u32[]{:S(2)}, u32[]{:S(2)}) collective-permute-start(f32[64,96]{1,0:T(8,128)S(1)} %get-tuple-element.98), channel_id=1, source_target_pairs={{1,0},{2,1},{3,2},{4,3},{5,4},{6,5},{7,6},{8,7},{9,8},{10,9},{11,1... | collective-permute-start | bytes 73736 | tf_op jit(solution)/shard_map/ppermute | solution.py:20
  25.9 7.7 %collective-permute-start.2 = (f32[64,96]{1,0:T(8,128)S(1)}, f32[64,96]{1,0:T(8,128)S(1)}, u32[]{:S(2)}, u32[]{:S(2)}) collective-permute-start(f32[64,96]{1,0:T(8,128)S(1)} %get-tuple-element.95), channel_id=1, source_target_pairs={{0,1},{1,2},{2,3},{3,4},{4,5},{5,6},{6,7},{7,8},{8,9},{9,10},{10,1... | collective-permute-start | bytes 73736 | tf_op jit(solution)/shard_map/ppermute | solution.py:19
  31.1 10.7 %collective-permute-start.3 = (f32[64,96]{1,0:T(8,128)S(1)}, f32[64,96]{1,0:T(8,128)S(1)}, u32[]{:S(2)}, u32[]{:S(2)}) collective-permute-start(f32[64,96]{1,0:T(8,128)S(1)} %get-tuple-element.96), channel_id=1, source_target_pairs={{1,0},{2,1},{3,2},{4,3},{5,4},{6,5},{7,6},{8,7},{9,8},{10,9},{11,1... | collective-permute-start | bytes 73736 | tf_op jit(solution)/shard_map/ppermute | solution.py:20
  91.7 7.7 %collective-permute-start.7 = (f32[6,96]{1,0:T(8,128)S(1)}, f32[6,96]{1,0:T(8,128)S(1)}, u32[]{:S(2)}, u32[]{:S(2)}) collective-permute-start(f32[6,96]{1,0:T(8,128)S(1)} %get-tuple-element.93), channel_id=1, source_target_pairs={{8,0},{16,8},{24,16},{32,24},{40,32},{48,40},{56,48},{64,56},{72,6... | collective-permute-start | bytes 6920 | tf_op jit(solution)/shard_map/ppermute | solution.py:20
  117.4 7.7 %collective-permute-start.9 = (f32[6,96]{1,0:T(8,128)S(1)}, f32[6,96]{1,0:T(8,128)S(1)}, u32[]{:S(2)}, u32[]{:S(2)}) collective-permute-start(f32[6,96]{1,0:T(8,128)S(1)} %get-tuple-element.91), channel_id=1, source_target_pairs={{8,0},{16,8},{24,16},{32,24},{40,32},{48,40},{56,48},{64,56},{72,6... | collective-permute-start | bytes 6920 | tf_op jit(solution)/shard_map/ppermute | solution.py:20
  231.5 7.7 %collective-permute-start.13 = (f32[6,96]{1,0:T(8,128)S(1)}, f32[6,96]{1,0:T(8,128)S(1)}, u32[]{:S(2)}, u32[]{:S(2)}) collective-permute-start(f32[6,96]{1,0:T(8,128)S(1)} %get-tuple-element.89), channel_id=1, source_target_pairs={{8,0},{16,8},{24,16},{32,24},{40,32},{48,40},{56,48},{64,56},{72,6... | collective-permute-start | bytes 6920 | tf_op jit(solution)/shard_map/ppermute | solution.py:20
  257.9 7.7 %collective-permute-start.15 = (f32[6,96]{1,0:T(8,128)S(1)}, f32[6,96]{1,0:T(8,128)S(1)}, u32[]{:S(2)}, u32[]{:S(2)}) collective-permute-start(f32[6,96]{1,0:T(8,128)S(1)} %get-tuple-element.87), channel_id=1, source_target_pairs={{8,0},{16,8},{24,16},{32,24},{40,32},{48,40},{56,48},{64,56},{72,6... | collective-permute-start | bytes 6920 | tf_op jit(solution)/shard_map/ppermute | solution.py:20
  285.7 7.7 %collective-permute-start.17 = (f32[6,96]{1,0:T(8,128)S(1)}, f32[6,96]{1,0:T(8,128)S(1)}, u32[]{:S(2)}, u32[]{:S(2)}) collective-permute-start(f32[6,96]{1,0:T(8,128)S(1)} %get-tuple-element.85), channel_id=1, source_target_pairs={{8,0},{16,8},{24,16},{32,24},{40,32},{48,40},{56,48},{64,56},{72,6... | collective-permute-start | bytes 6920 | tf_op jit(solution)/shard_map/ppermute | solution.py:20
  299.4 40.1 %collective-permute-start.18 = (f32[64,96]{1,0:T(8,128)S(1)}, f32[64,96]{1,0:T(8,128)S(1)}, u32[]{:S(2)}, u32[]{:S(2)}) collective-permute-start(f32[64,96]{1,0:T(8,128)S(1)} %get-tuple-element.83), channel_id=1, source_target_pairs={{0,1},{1,2},{2,3},{3,4},{4,5},{5,6},{6,7},{7,8},{8,9},{9,10},{10,1... | collective-permute-start | bytes 73736 | tf_op jit(solution)/shard_map/ppermute | solution.py:19
  337.4 10.7 %collective-permute-start.19 = (f32[64,96]{1,0:T(8,128)S(1)}, f32[64,96]{1,0:T(8,128)S(1)}, u32[]{:S(2)}, u32[]{:S(2)}) collective-permute-start(f32[64,96]{1,0:T(8,128)S(1)} %get-tuple-element.84), channel_id=1, source_target_pairs={{1,0},{2,1},{3,2},{4,3},{5,4},{6,5},{7,6},{8,7},{9,8},{10,9},{11,1... | collective-permute-start | bytes 73736 | tf_op jit(solution)/shard_map/ppermute | solution.py:20
  355.4 10.7 %collective-permute-start.21 = (f32[64,96]{1,0:T(8,128)S(1)}, f32[64,96]{1,0:T(8,128)S(1)}, u32[]{:S(2)}, u32[]{:S(2)}) collective-permute-start(f32[64,96]{1,0:T(8,128)S(1)} %get-tuple-element.82), channel_id=1, source_target_pairs={{1,0},{2,1},{3,2},{4,3},{5,4},{6,5},{7,6},{8,7},{9,8},{10,9},{11,1... | collective-permute-start | bytes 73736 | tf_op jit(solution)/shard_map/ppermute | solution.py:20
  373.3 10.7 %collective-permute-start.23 = (f32[64,96]{1,0:T(8,128)S(1)}, f32[64,96]{1,0:T(8,128)S(1)}, u32[]{:S(2)}, u32[]{:S(2)}) collective-permute-start(f32[64,96]{1,0:T(8,128)S(1)} %get-tuple-element.80), channel_id=1, source_target_pairs={{1,0},{2,1},{3,2},{4,3},{5,4},{6,5},{7,6},{8,7},{9,8},{10,9},{11,1... | collective-permute-start | bytes 73736 | tf_op jit(solution)/shard_map/ppermute | solution.py:20
  394.3 10.7 %collective-permute-start.25 = (f32[64,96]{1,0:T(8,128)S(1)}, f32[64,96]{1,0:T(8,128)S(1)}, u32[]{:S(2)}, u32[]{:S(2)}) collective-permute-start(f32[64,96]{1,0:T(8,128)S(1)} %get-tuple-element.78), channel_id=1, source_target_pairs={{1,0},{2,1},{3,2},{4,3},{5,4},{6,5},{7,6},{8,7},{9,8},{10,9},{11,1... | collective-permute-start | bytes 73736 | tf_op jit(solution)/shard_map/ppermute | solution.py:20
  415.3 10.7 %collective-permute-start.27 = (f32[64,96]{1,0:T(8,128)S(1)}, f32[64,96]{1,0:T(8,128)S(1)}, u32[]{:S(2)}, u32[]{:S(2)}) collective-permute-start(f32[64,96]{1,0:T(8,128)S(1)} %get-tuple-element.76), channel_id=1, source_target_pairs={{1,0},{2,1},{3,2},{4,3},{5,4},{6,5},{7,6},{8,7},{9,8},{10,9},{11,1... | collective-permute-start | bytes 73736 | tf_op jit(solution)/shard_map/ppermute | solution.py:20
  466.6 7.7 %collective-permute-start.29 = (f32[6,96]{1,0:T(8,128)S(1)}, f32[6,96]{1,0:T(8,128)S(1)}, u32[]{:S(2)}, u32[]{:S(2)}) collective-permute-start(f32[6,96]{1,0:T(8,128)S(1)} %get-tuple-element.57), channel_id=1, source_target_pairs={{8,0},{16,8},{24,16},{32,24},{40,32},{48,40},{56,48},{64,56},{72,6... | collective-permute-start | bytes 6920 | tf_op jit(solution)/shard_map/ppermute | solution.py:28
  476.6 7.7 %collective-permute-start.31 = (f32[6,96]{1,0:T(8,128)S(1)}, f32[6,96]{1,0:T(8,128)S(1)}, u32[]{:S(2)}, u32[]{:S(2)}) collective-permute-start(f32[6,96]{1,0:T(8,128)S(1)} %get-tuple-element.73), channel_id=1, source_target_pairs={{8,0},{16,8},{24,16},{32,24},{40,32},{48,40},{56,48},{64,56},{72,6... | collective-permute-start | bytes 6920 | tf_op jit(solution)/shard_map/ppermute | solution.py:20
  502.9 7.7 %collective-permute-start.33 = (f32[6,96]{1,0:T(8,128)S(1)}, f32[6,96]{1,0:T(8,128)S(1)}, u32[]{:S(2)}, u32[]{:S(2)}) collective-permute-start(f32[6,96]{1,0:T(8,128)S(1)} %get-tuple-element.71), channel_id=1, source_target_pairs={{8,0},{16,8},{24,16},{32,24},{40,32},{48,40},{56,48},{64,56},{72,6... | collective-permute-start | bytes 6920 | tf_op jit(solution)/shard_map/ppermute | solution.py:20
  618.7 7.7 %collective-permute-start.37 = (f32[6,96]{1,0:T(8,128)S(1)}, f32[6,96]{1,0:T(8,128)S(1)}, u32[]{:S(2)}, u32[]{:S(2)}) collective-permute-start(f32[6,96]{1,0:T(8,128)S(1)} %get-tuple-element.69), channel_id=1, source_target_pairs={{8,0},{16,8},{24,16},{32,24},{40,32},{48,40},{56,48},{64,56},{72,6... | collective-permute-start | bytes 6920 | tf_op jit(solution)/shard_map/ppermute | solution.py:20
  645.1 7.7 %collective-permute-start.39 = (f32[6,96]{1,0:T(8,128)S(1)}, f32[6,96]{1,0:T(8,128)S(1)}, u32[]{:S(2)}, u32[]{:S(2)}) collective-permute-start(f32[6,96]{1,0:T(8,128)S(1)} %get-tuple-element.67), channel_id=1, source_target_pairs={{8,0},{16,8},{24,16},{32,24},{40,32},{48,40},{56,48},{64,56},{72,6... | collective-permute-start | bytes 6920 | tf_op jit(solution)/shard_map/ppermute | solution.py:20
  672.9 7.7 %collective-permute-start.41 = (f32[6,96]{1,0:T(8,128)S(1)}, f32[6,96]{1,0:T(8,128)S(1)}, u32[]{:S(2)}, u32[]{:S(2)}) collective-permute-start(f32[6,96]{1,0:T(8,128)S(1)} %get-tuple-element.65), channel_id=1, source_target_pairs={{8,0},{16,8},{24,16},{32,24},{40,32},{48,40},{56,48},{64,56},{72,6... | collective-permute-start | bytes 6920 | tf_op jit(solution)/shard_map/ppermute | solution.py:20
  686.5 40.0 %collective-permute-start.42 = (f32[64,96]{1,0:T(8,128)S(1)}, f32[64,96]{1,0:T(8,128)S(1)}, u32[]{:S(2)}, u32[]{:S(2)}) collective-permute-start(f32[64,96]{1,0:T(8,128)S(1)} %get-tuple-element.63), channel_id=1, source_target_pairs={{0,1},{1,2},{2,3},{3,4},{4,5},{5,6},{6,7},{7,8},{8,9},{9,10},{10,1... | collective-permute-start | bytes 73736 | tf_op jit(solution)/shard_map/ppermute | solution.py:19
  724.6 10.7 %collective-permute-start.43 = (f32[64,96]{1,0:T(8,128)S(1)}, f32[64,96]{1,0:T(8,128)S(1)}, u32[]{:S(2)}, u32[]{:S(2)}) collective-permute-start(f32[64,96]{1,0:T(8,128)S(1)} %get-tuple-element.64), channel_id=1, source_target_pairs={{1,0},{2,1},{3,2},{4,3},{5,4},{6,5},{7,6},{8,7},{9,8},{10,9},{11,1... | collective-permute-start | bytes 73736 | tf_op jit(solution)/shard_map/ppermute | solution.py:20
  742.5 10.7 %collective-permute-start.45 = (f32[64,96]{1,0:T(8,128)S(1)}, f32[64,96]{1,0:T(8,128)S(1)}, u32[]{:S(2)}, u32[]{:S(2)}) collective-permute-start(f32[64,96]{1,0:T(8,128)S(1)} %get-tuple-element.62), channel_id=1, source_target_pairs={{1,0},{2,1},{3,2},{4,3},{5,4},{6,5},{7,6},{8,7},{9,8},{10,9},{11,1... | collective-permute-start | bytes 73736 | tf_op jit(solution)/shard_map/ppermute | solution.py:20
  (39 other events, 689.8 us)
where the time goes:
time: 763 us; the launch traced here: 759 us
  local copies, waits for them, and re-layouts  195 us (26%)
  blocking collectives  192 us (25%)
  starting transfers between devices  191 us (25%)
  waiting for transfers between devices  131 us (17%)
  other arithmetic  49.2 us (6%)
    all_gather x2, blocking collectives, shards(): every = lax.all_gather(parts[None], 'slab', axis=0, tiled=True)  144 us
    ppermute x21, waiting for transfers between devices, padded(): after = lax.ppermute(leading, axis, down)  124 us
    ppermute x21, starting transfers between devices, padded(): before = lax.ppermute(last, axis, up)  123 us
    gather x17, local copies, waits for them, and re-layouts, apply_local(): picked = jnp.swapaxes(extended[:, local_cols], 0, 1)  115 us
    ppermute x21, starting transfers between devices, padded(): after = lax.ppermute(leading, axis, down)  57.4 us
    psum x2, blocking collectives, shards(): partial_sum = lax.psum(partial_sum, 'sec')  48.3 us
    transpose x17, local copies, waits for them, and re-layouts, apply_local(): picked = jnp.swapaxes(extended[:, local_cols], 0, 1)  30.7 us
    concatenate x29, local copies, waits for them, and re-layouts, padded(): array = jnp.concatenate([before, array, after], axis=dim)  25 us
  transfers between devices with their start and end apart: 46, of which 23 were waited for; matrix products, arithmetic and copies ran while one was open for 1% of the time, Pallas kernels for 0%

commit v1 on v0

--- a/solution.py
+++ b/solution.py
@@ -100,7 +100,8 @@
         coarse_res = coarse_rhs - coarse_apply(coarse_sol)
         parts = jnp.sum(section_prolong * coarse_res[None, :, None, :], axis=(1, 3))
         width = parts.shape[1]
-        every = lax.all_gather(parts[None], "slab", axis=0, tiled=True)
+        copies = jnp.concatenate([parts[None]] * lax.axis_size("slab"), axis=0)
+        every = lax.all_to_all(copies, "slab", 0, 0, tiled=True)
         zero = jnp.zeros((1, width), jnp.float32)
         total = (
             every[:, 1]

time: 763 us -> 617 us (0.81)
  blocking collectives: 192 us -> 94 us
  starting transfers between devices: 191 us -> 141 us
    all_gather x2 -> x0, blocking collectives: 144 us -> none  [shards(): every = lax.all_gather(parts[None], 'slab', axis=0, tiled=True)]
    ppermute x21, starting transfers between devices: 123 us -> 73.4 us  [padded(): before = lax.ppermute(last, axis, up)]
    all_to_all x0 -> x2, blocking collectives: none -> 45.7 us  [shards(): every = lax.all_to_all(copies, 'slab', 0, 0, tiled=True)]
  transfers between devices with their start and end apart: 46 -> 46, of which waited for: 23 -> 23; matrix products, arithmetic and copies ran while one was open for 1% -> 2% of each run, Pallas kernels for 0% -> 0%
where the time goes in v1:
time: 617 us; the launch traced here: 613 us
  local copies, waits for them, and re-layouts  196 us (32%)
  starting transfers between devices  141 us (23%)
  waiting for transfers between devices  131 us (21%)
  blocking collectives  94 us (15%)
  other arithmetic  49.2 us (8%)
    ppermute x21, waiting for transfers between devices, padded(): after = lax.ppermute(leading, axis, down)  124 us
    gather x17, local copies, waits for them, and re-layouts, apply_local(): picked = jnp.swapaxes(extended[:, local_cols], 0, 1)  115 us
    ppermute x21, starting transfers between devices, padded(): before = lax.ppermute(last, axis, up)  73.4 us
    ppermute x21, starting transfers between devices, padded(): after = lax.ppermute(leading, axis, down)  57.6 us
    psum x2, blocking collectives, shards(): partial_sum = lax.psum(partial_sum, 'sec')  48.3 us
    all_to_all x2, blocking collectives, shards(): every = lax.all_to_all(copies, 'slab', 0, 0, tiled=True)  45.7 us
    transpose x17, local copies, waits for them, and re-layouts, apply_local(): picked = jnp.swapaxes(extended[:, local_cols], 0, 1)  30.7 us
    concatenate x29, local copies, waits for them, and re-layouts, padded(): array = jnp.concatenate([before, array, after], axis=dim)  25 us
  transfers between devices with their start and end apart: 46, of which 23 were waited for; matrix products, arithmetic and copies ran while one was open for 2% of the time, Pallas kernels for 0%

profile of v1, /device:TPU:127, one launch (start us, length us, event | category | flops | bytes accessed | tf_op | source)
XLA Modules:
  0.0 612.6 jit_solution(1167036647755247599)
XLA Ops:
  33.6 8.1 %collective-permute-done.3 = f32[64,96]{1,0:T(8,128)S(1)} collective-permute-done((f32[64,96]{1,0:T(8,128)S(1)}, f32[64,96]{1,0:T(8,128)S(1)}, u32[]{:S(2)}, u32[]{:S(2)}) %collective-permute-start.3) | collective-permute-done | bytes 24608 | tf_op jit(solution)/shard_map/ppermute | solution.py:20
  53.9 23.9 %psum.14 = f32[6,1216]{1,0:T(8,128)S(1)} all-reduce(f32[6,1216]{1,0:T(8,128)S(1)} %copy.149), channel_id=1, replica_groups=mesh['slab'=64,'sec'=8] {'sec'}, use_global_device_ids=true, to_apply=%region_4.5 | all-reduce | flops 7296 | bytes 58368 | tf_op jit(solution)/shard_map/psum | solution.py:94
  100.5 11.9 %gather_fusion.4 = f32[3072,6]{1,0:T(8,128)} fusion(f32[6,1216]{0,1:T(8,128)} %copy.150, s32[3072]{0:T(1024)S(1)} %broadcast_clamp_fusion), kind=kCustom, calls=%fused_computation.4 | custom fusion | bytes 159744 | tf_op jit(solution)/shard_map/gather | solution.py:36
  126.3 11.9 %gather_fusion.5 = f32[3072,6]{1,0:T(8,128)} fusion(f32[6,1216]{0,1:T(8,128)} %copy.152, s32[3072]{0:T(1024)S(1)} %broadcast_clamp_fusion), kind=kCustom, calls=%fused_computation.5 | custom fusion | bytes 159744 | tf_op jit(solution)/shard_map/gather | solution.py:36
  142.7 24.9 %all_to_all.10 = f32[64,3,24]{2,1,0:T(4,128)S(1)} all-to-all(f32[64,3,24]{2,1,0:T(4,128)S(1)} %concatenate.103), channel_id=1, replica_groups=mesh['slab'=64,'sec'=8] {'slab'}, dimensions={0} | all-to-all | bytes 36864 | tf_op jit(solution)/shard_map/all_to_all | solution.py:104
  175.7 5.7 collective-permute-done.11
  193.7 11.9 %gather_fusion.6 = f32[3072,6]{1,0:T(8,128)} fusion(f32[6,1216]{0,1:T(8,128)} %copy.158, s32[3072]{0:T(1024)S(1)} %broadcast_clamp_fusion), kind=kCustom, calls=%fused_computation.6 | custom fusion | bytes 159744 | tf_op jit(solution)/shard_map/gather | solution.py:36
  221.5 11.9 %gather_fusion.7 = f32[3072,6]{1,0:T(8,128)} fusion(f32[6,1216]{0,1:T(8,128)} %copy.160, s32[3072]{0:T(1024)S(1)} %broadcast_clamp_fusion), kind=kCustom, calls=%fused_computation.7 | custom fusion | bytes 159744 | tf_op jit(solution)/shard_map/gather | solution.py:36
  252.7 13.5 %collective-permute-start.18 = (f32[64,96]{1,0:T(8,128)S(1)}, f32[64,96]{1,0:T(8,128)S(1)}, u32[]{:S(2)}, u32[]{:S(2)}) collective-permute-start(f32[64,96]{1,0:T(8,128)S(1)} %get-tuple-element.83), channel_id=1, source_target_pairs={{0,1},{1,2},{2,3},{3,4},{4,5},{5,6},{6,7},{7,8},{8,9},{9,10},{10,1... | collective-permute-start | bytes 73736 | tf_op jit(solution)/shard_map/ppermute | solution.py:19
  268.1 8.7 %collective-permute-done.19 = f32[64,96]{1,0:T(8,128)S(1)} collective-permute-done((f32[64,96]{1,0:T(8,128)S(1)}, f32[64,96]{1,0:T(8,128)S(1)}, u32[]{:S(2)}, u32[]{:S(2)}) %collective-permute-start.19) | collective-permute-done | bytes 24608 | tf_op jit(solution)/shard_map/ppermute | solution.py:20
  286.5 8.2 %collective-permute-done.21 = f32[64,96]{1,0:T(8,128)S(1)} collective-permute-done((f32[64,96]{1,0:T(8,128)S(1)}, f32[64,96]{1,0:T(8,128)S(1)}, u32[]{:S(2)}, u32[]{:S(2)}) %collective-permute-start.21) | collective-permute-done | bytes 24608 | tf_op jit(solution)/shard_map/ppermute | solution.py:20
  304.5 8.2 %collective-permute-done.23 = f32[64,96]{1,0:T(8,128)S(1)} collective-permute-done((f32[64,96]{1,0:T(8,128)S(1)}, f32[64,96]{1,0:T(8,128)S(1)}, u32[]{:S(2)}, u32[]{:S(2)}) %collective-permute-start.23) | collective-permute-done | bytes 24608 | tf_op jit(solution)/shard_map/ppermute | solution.py:20
  325.5 8.2 %collective-permute-done.25 = f32[64,96]{1,0:T(8,128)S(1)} collective-permute-done((f32[64,96]{1,0:T(8,128)S(1)}, f32[64,96]{1,0:T(8,128)S(1)}, u32[]{:S(2)}, u32[]{:S(2)}) %collective-permute-start.25) | collective-permute-done | bytes 24608 | tf_op jit(solution)/shard_map/ppermute | solution.py:20
  346.4 8.2 %collective-permute-done.27 = f32[64,96]{1,0:T(8,128)S(1)} collective-permute-done((f32[64,96]{1,0:T(8,128)S(1)}, f32[64,96]{1,0:T(8,128)S(1)}, u32[]{:S(2)}, u32[]{:S(2)}) %collective-permute-start.27) | collective-permute-done | bytes 24608 | tf_op jit(solution)/shard_map/ppermute | solution.py:20
  368.9 24.5 %psum.15 = f32[6,1216]{1,0:T(8,128)S(1)} all-reduce(f32[6,1216]{1,0:T(8,128)} %copy.175), channel_id=1, replica_groups=mesh['slab'=64,'sec'=8] {'sec'}, use_global_device_ids=true, to_apply=%region_20.21 | all-reduce | flops 7296 | bytes 58368 | tf_op jit(solution)/shard_map/psum | solution.py:94
  414.2 11.9 %gather_fusion.14 = f32[3072,6]{1,0:T(8,128)} fusion(f32[6,1216]{0,1:T(8,128)} %copy.176, s32[3072]{0:T(1024)S(1)} %broadcast_clamp_fusion), kind=kCustom, calls=%fused_computation.14 | custom fusion | bytes 159744 | tf_op jit(solution)/shard_map/gather | solution.py:36
  440.5 11.9 %gather_fusion.15 = f32[3072,6]{1,0:T(8,128)} fusion(f32[6,1216]{0,1:T(8,128)} %copy.178, s32[3072]{0:T(1024)S(1)} %broadcast_clamp_fusion), kind=kCustom, calls=%fused_computation.15 | custom fusion | bytes 159744 | tf_op jit(solution)/shard_map/gather | solution.py:36
  457.5 20.8 %all_to_all.11 = f32[64,3,24]{2,1,0:T(4,128)S(1)} all-to-all(f32[64,3,24]{2,1,0:T(4,128)S(1)} %concatenate.117), channel_id=1, replica_groups=mesh['slab'=64,'sec'=8] {'slab'}, dimensions={0} | all-to-all | bytes 36864 | tf_op jit(solution)/shard_map/all_to_all | solution.py:104
  487.8 5.7 collective-permute-done.35
  505.8 11.9 %gather_fusion.16 = f32[3072,6]{1,0:T(8,128)} fusion(f32[6,1216]{0,1:T(8,128)} %copy.184, s32[3072]{0:T(1024)S(1)} %broadcast_clamp_fusion), kind=kCustom, calls=%fused_computation.16 | custom fusion | bytes 159744 | tf_op jit(solution)/shard_map/gather | solution.py:36
  533.5 11.9 %gather_fusion.17 = f32[3072,6]{1,0:T(8,128)} fusion(f32[6,1216]{0,1:T(8,128)} %copy.186, s32[3072]{0:T(1024)S(1)} %broadcast_clamp_fusion), kind=kCustom, calls=%fused_computation.17 | custom fusion | bytes 159744 | tf_op jit(solution)/shard_map/gather | solution.py:36
  564.7 13.5 %collective-permute-start.42 = (f32[64,96]{1,0:T(8,128)S(1)}, f32[64,96]{1,0:T(8,128)S(1)}, u32[]{:S(2)}, u32[]{:S(2)}) collective-permute-start(f32[64,96]{1,0:T(8,128)S(1)} %get-tuple-element.63), channel_id=1, source_target_pairs={{0,1},{1,2},{2,3},{3,4},{4,5},{5,6},{6,7},{7,8},{8,9},{9,10},{10,1... | collective-permute-start | bytes 73736 | tf_op jit(solution)/shard_map/ppermute | solution.py:19
  580.1 8.7 %collective-permute-done.43 = f32[64,96]{1,0:T(8,128)S(1)} collective-permute-done((f32[64,96]{1,0:T(8,128)S(1)}, f32[64,96]{1,0:T(8,128)S(1)}, u32[]{:S(2)}, u32[]{:S(2)}) %collective-permute-start.43) | collective-permute-done | bytes 24608 | tf_op jit(solution)/shard_map/ppermute | solution.py:20
  598.5 8.2 %collective-permute-done.45 = f32[64,96]{1,0:T(8,128)S(1)} collective-permute-done((f32[64,96]{1,0:T(8,128)S(1)}, f32[64,96]{1,0:T(8,128)S(1)}, u32[]{:S(2)}, u32[]{:S(2)}) %collective-permute-start.45) | collective-permute-done | bytes 24608 | tf_op jit(solution)/shard_map/ppermute | solution.py:20
  (309 shorter events, 317.3 us)
Async XLA Ops:
  4.9 11.6 %collective-permute-start = (f32[64,96]{1,0:T(8,128)S(1)}, f32[64,96]{1,0:T(8,128)S(1)}, u32[]{:S(2)}, u32[]{:S(2)}) collective-permute-start(f32[64,96]{1,0:T(8,128)S(1)} %get-tuple-element.97), channel_id=1, source_target_pairs={{0,1},{1,2},{2,3},{3,4},{4,5},{5,6},{6,7},{7,8},{8,9},{9,10},{10,1... | collective-permute-start | bytes 73736 | tf_op jit(solution)/shard_map/ppermute | solution.py:19
  9.8 10.7 %collective-permute-start.1 = (f32[64,96]{1,0:T(8,128)S(1)}, f32[64,96]{1,0:T(8,128)S(1)}, u32[]{:S(2)}, u32[]{:S(2)}) collective-permute-start(f32[64,96]{1,0:T(8,128)S(1)} %get-tuple-element.98), channel_id=1, source_target_pairs={{1,0},{2,1},{3,2},{4,3},{5,4},{6,5},{7,6},{8,7},{9,8},{10,9},{11,1... | collective-permute-start | bytes 73736 | tf_op jit(solution)/shard_map/ppermute | solution.py:20
  25.9 7.7 %collective-permute-start.2 = (f32[64,96]{1,0:T(8,128)S(1)}, f32[64,96]{1,0:T(8,128)S(1)}, u32[]{:S(2)}, u32[]{:S(2)}) collective-permute-start(f32[64,96]{1,0:T(8,128)S(1)} %get-tuple-element.95), channel_id=1, source_target_pairs={{0,1},{1,2},{2,3},{3,4},{4,5},{5,6},{6,7},{7,8},{8,9},{9,10},{10,1... | collective-permute-start | bytes 73736 | tf_op jit(solution)/shard_map/ppermute | solution.py:19
  31.1 10.7 %collective-permute-start.3 = (f32[64,96]{1,0:T(8,128)S(1)}, f32[64,96]{1,0:T(8,128)S(1)}, u32[]{:S(2)}, u32[]{:S(2)}) collective-permute-start(f32[64,96]{1,0:T(8,128)S(1)} %get-tuple-element.96), channel_id=1, source_target_pairs={{1,0},{2,1},{3,2},{4,3},{5,4},{6,5},{7,6},{8,7},{9,8},{10,9},{11,1... | collective-permute-start | bytes 73736 | tf_op jit(solution)/shard_map/ppermute | solution.py:20
  91.7 7.7 %collective-permute-start.7 = (f32[6,96]{1,0:T(8,128)S(1)}, f32[6,96]{1,0:T(8,128)S(1)}, u32[]{:S(2)}, u32[]{:S(2)}) collective-permute-start(f32[6,96]{1,0:T(8,128)S(1)} %get-tuple-element.93), channel_id=1, source_target_pairs={{8,0},{16,8},{24,16},{32,24},{40,32},{48,40},{56,48},{64,56},{72,6... | collective-permute-start | bytes 6920 | tf_op jit(solution)/shard_map/ppermute | solution.py:20
  117.4 7.7 %collective-permute-start.9 = (f32[6,96]{1,0:T(8,128)S(1)}, f32[6,96]{1,0:T(8,128)S(1)}, u32[]{:S(2)}, u32[]{:S(2)}) collective-permute-start(f32[6,96]{1,0:T(8,128)S(1)} %get-tuple-element.91), channel_id=1, source_target_pairs={{8,0},{16,8},{24,16},{32,24},{40,32},{48,40},{56,48},{64,56},{72,6... | collective-permute-start | bytes 6920 | tf_op jit(solution)/shard_map/ppermute | solution.py:20
  184.8 7.7 %collective-permute-start.13 = (f32[6,96]{1,0:T(8,128)S(1)}, f32[6,96]{1,0:T(8,128)S(1)}, u32[]{:S(2)}, u32[]{:S(2)}) collective-permute-start(f32[6,96]{1,0:T(8,128)S(1)} %get-tuple-element.89), channel_id=1, source_target_pairs={{8,0},{16,8},{24,16},{32,24},{40,32},{48,40},{56,48},{64,56},{72,6... | collective-permute-start | bytes 6920 | tf_op jit(solution)/shard_map/ppermute | solution.py:20
  211.2 7.7 %collective-permute-start.15 = (f32[6,96]{1,0:T(8,128)S(1)}, f32[6,96]{1,0:T(8,128)S(1)}, u32[]{:S(2)}, u32[]{:S(2)}) collective-permute-start(f32[6,96]{1,0:T(8,128)S(1)} %get-tuple-element.87), channel_id=1, source_target_pairs={{8,0},{16,8},{24,16},{32,24},{40,32},{48,40},{56,48},{64,56},{72,6... | collective-permute-start | bytes 6920 | tf_op jit(solution)/shard_map/ppermute | solution.py:20
  239.0 7.7 %collective-permute-start.17 = (f32[6,96]{1,0:T(8,128)S(1)}, f32[6,96]{1,0:T(8,128)S(1)}, u32[]{:S(2)}, u32[]{:S(2)}) collective-permute-start(f32[6,96]{1,0:T(8,128)S(1)} %get-tuple-element.85), channel_id=1, source_target_pairs={{8,0},{16,8},{24,16},{32,24},{40,32},{48,40},{56,48},{64,56},{72,6... | collective-permute-start | bytes 6920 | tf_op jit(solution)/shard_map/ppermute | solution.py:20
  252.7 15.4 %collective-permute-start.18 = (f32[64,96]{1,0:T(8,128)S(1)}, f32[64,96]{1,0:T(8,128)S(1)}, u32[]{:S(2)}, u32[]{:S(2)}) collective-permute-start(f32[64,96]{1,0:T(8,128)S(1)} %get-tuple-element.83), channel_id=1, source_target_pairs={{0,1},{1,2},{2,3},{3,4},{4,5},{5,6},{6,7},{7,8},{8,9},{9,10},{10,1... | collective-permute-start | bytes 73736 | tf_op jit(solution)/shard_map/ppermute | solution.py:19
  266.2 10.7 %collective-permute-start.19 = (f32[64,96]{1,0:T(8,128)S(1)}, f32[64,96]{1,0:T(8,128)S(1)}, u32[]{:S(2)}, u32[]{:S(2)}) collective-permute-start(f32[64,96]{1,0:T(8,128)S(1)} %get-tuple-element.84), channel_id=1, source_target_pairs={{1,0},{2,1},{3,2},{4,3},{5,4},{6,5},{7,6},{8,7},{9,8},{10,9},{11,1... | collective-permute-start | bytes 73736 | tf_op jit(solution)/shard_map/ppermute | solution.py:20
  284.1 10.7 %collective-permute-start.21 = (f32[64,96]{1,0:T(8,128)S(1)}, f32[64,96]{1,0:T(8,128)S(1)}, u32[]{:S(2)}, u32[]{:S(2)}) collective-permute-start(f32[64,96]{1,0:T(8,128)S(1)} %get-tuple-element.82), channel_id=1, source_target_pairs={{1,0},{2,1},{3,2},{4,3},{5,4},{6,5},{7,6},{8,7},{9,8},{10,9},{11,1... | collective-permute-start | bytes 73736 | tf_op jit(solution)/shard_map/ppermute | solution.py:20
  302.1 10.7 %collective-permute-start.23 = (f32[64,96]{1,0:T(8,128)S(1)}, f32[64,96]{1,0:T(8,128)S(1)}, u32[]{:S(2)}, u32[]{:S(2)}) collective-permute-start(f32[64,96]{1,0:T(8,128)S(1)} %get-tuple-element.80), channel_id=1, source_target_pairs={{1,0},{2,1},{3,2},{4,3},{5,4},{6,5},{7,6},{8,7},{9,8},{10,9},{11,1... | collective-permute-start | bytes 73736 | tf_op jit(solution)/shard_map/ppermute | solution.py:20
  323.0 10.7 %collective-permute-start.25 = (f32[64,96]{1,0:T(8,128)S(1)}, f32[64,96]{1,0:T(8,128)S(1)}, u32[]{:S(2)}, u32[]{:S(2)}) collective-permute-start(f32[64,96]{1,0:T(8,128)S(1)} %get-tuple-element.78), channel_id=1, source_target_pairs={{1,0},{2,1},{3,2},{4,3},{5,4},{6,5},{7,6},{8,7},{9,8},{10,9},{11,1... | collective-permute-start | bytes 73736 | tf_op jit(solution)/shard_map/ppermute | solution.py:20
  344.0 10.7 %collective-permute-start.27 = (f32[64,96]{1,0:T(8,128)S(1)}, f32[64,96]{1,0:T(8,128)S(1)}, u32[]{:S(2)}, u32[]{:S(2)}) collective-permute-start(f32[64,96]{1,0:T(8,128)S(1)} %get-tuple-element.76), channel_id=1, source_target_pairs={{1,0},{2,1},{3,2},{4,3},{5,4},{6,5},{7,6},{8,7},{9,8},{10,9},{11,1... | collective-permute-start | bytes 73736 | tf_op jit(solution)/shard_map/ppermute | solution.py:20
  395.4 7.7 %collective-permute-start.29 = (f32[6,96]{1,0:T(8,128)S(1)}, f32[6,96]{1,0:T(8,128)S(1)}, u32[]{:S(2)}, u32[]{:S(2)}) collective-permute-start(f32[6,96]{1,0:T(8,128)S(1)} %get-tuple-element.57), channel_id=1, source_target_pairs={{8,0},{16,8},{24,16},{32,24},{40,32},{48,40},{56,48},{64,56},{72,6... | collective-permute-start | bytes 6920 | tf_op jit(solution)/shard_map/ppermute | solution.py:28
  405.3 7.7 %collective-permute-start.31 = (f32[6,96]{1,0:T(8,128)S(1)}, f32[6,96]{1,0:T(8,128)S(1)}, u32[]{:S(2)}, u32[]{:S(2)}) collective-permute-start(f32[6,96]{1,0:T(8,128)S(1)} %get-tuple-element.73), channel_id=1, source_target_pairs={{8,0},{16,8},{24,16},{32,24},{40,32},{48,40},{56,48},{64,56},{72,6... | collective-permute-start | bytes 6920 | tf_op jit(solution)/shard_map/ppermute | solution.py:20
  431.7 7.7 %collective-permute-start.33 = (f32[6,96]{1,0:T(8,128)S(1)}, f32[6,96]{1,0:T(8,128)S(1)}, u32[]{:S(2)}, u32[]{:S(2)}) collective-permute-start(f32[6,96]{1,0:T(8,128)S(1)} %get-tuple-element.71), channel_id=1, source_target_pairs={{8,0},{16,8},{24,16},{32,24},{40,32},{48,40},{56,48},{64,56},{72,6... | collective-permute-start | bytes 6920 | tf_op jit(solution)/shard_map/ppermute | solution.py:20
  496.9 7.7 %collective-permute-start.37 = (f32[6,96]{1,0:T(8,128)S(1)}, f32[6,96]{1,0:T(8,128)S(1)}, u32[]{:S(2)}, u32[]{:S(2)}) collective-permute-start(f32[6,96]{1,0:T(8,128)S(1)} %get-tuple-element.69), channel_id=1, source_target_pairs={{8,0},{16,8},{24,16},{32,24},{40,32},{48,40},{56,48},{64,56},{72,6... | collective-permute-start | bytes 6920 | tf_op jit(solution)/shard_map/ppermute | solution.py:20
  523.3 7.7 %collective-permute-start.39 = (f32[6,96]{1,0:T(8,128)S(1)}, f32[6,96]{1,0:T(8,128)S(1)}, u32[]{:S(2)}, u32[]{:S(2)}) collective-permute-start(f32[6,96]{1,0:T(8,128)S(1)} %get-tuple-element.67), channel_id=1, source_target_pairs={{8,0},{16,8},{24,16},{32,24},{40,32},{48,40},{56,48},{64,56},{72,6... | collective-permute-start | bytes 6920 | tf_op jit(solution)/shard_map/ppermute | solution.py:20
  551.1 7.7 %collective-permute-start.41 = (f32[6,96]{1,0:T(8,128)S(1)}, f32[6,96]{1,0:T(8,128)S(1)}, u32[]{:S(2)}, u32[]{:S(2)}) collective-permute-start(f32[6,96]{1,0:T(8,128)S(1)} %get-tuple-element.65), channel_id=1, source_target_pairs={{8,0},{16,8},{24,16},{32,24},{40,32},{48,40},{56,48},{64,56},{72,6... | collective-permute-start | bytes 6920 | tf_op jit(solution)/shard_map/ppermute | solution.py:20
  564.7 15.4 %collective-permute-start.42 = (f32[64,96]{1,0:T(8,128)S(1)}, f32[64,96]{1,0:T(8,128)S(1)}, u32[]{:S(2)}, u32[]{:S(2)}) collective-permute-start(f32[64,96]{1,0:T(8,128)S(1)} %get-tuple-element.63), channel_id=1, source_target_pairs={{0,1},{1,2},{2,3},{3,4},{4,5},{5,6},{6,7},{7,8},{8,9},{9,10},{10,1... | collective-permute-start | bytes 73736 | tf_op jit(solution)/shard_map/ppermute | solution.py:19
  578.2 10.7 %collective-permute-start.43 = (f32[64,96]{1,0:T(8,128)S(1)}, f32[64,96]{1,0:T(8,128)S(1)}, u32[]{:S(2)}, u32[]{:S(2)}) collective-permute-start(f32[64,96]{1,0:T(8,128)S(1)} %get-tuple-element.64), channel_id=1, source_target_pairs={{1,0},{2,1},{3,2},{4,3},{5,4},{6,5},{7,6},{8,7},{9,8},{10,9},{11,1... | collective-permute-start | bytes 73736 | tf_op jit(solution)/shard_map/ppermute | solution.py:20
  596.1 10.7 %collective-permute-start.45 = (f32[64,96]{1,0:T(8,128)S(1)}, f32[64,96]{1,0:T(8,128)S(1)}, u32[]{:S(2)}, u32[]{:S(2)}) collective-permute-start(f32[64,96]{1,0:T(8,128)S(1)} %get-tuple-element.62), channel_id=1, source_target_pairs={{1,0},{2,1},{3,2},{4,3},{5,4},{6,5},{7,6},{8,7},{9,8},{10,9},{11,1... | collective-permute-start | bytes 73736 | tf_op jit(solution)/shard_map/ppermute | solution.py:20
  (41 other events, 595.5 us)
